TPU v7x, 32 devices: a whole 2x2x4 slice. The times are simulated.
32 devices in a mesh: sp: 8 (over y, x, core), tp: 4 (over z).
Axes of the slice: x: 2, y: 2, z: 4, core: 2. Of those that a mesh axis runs over, the one named last changes fastest.
Arguments:
- queries: bfloat16 [4096, 8192], P('sp', 'tp'), may hold values from -200 to 200
- keys: bfloat16 [4096, 1024], P('sp', 'tp'), may hold values from -6 to 6
- values: bfloat16 [4096, 1024], P('sp', 'tp'), may hold values from -6 to 6
- w_out: bfloat16 [8192, 4096], P('tp'), may hold values from -0.0625 to 0.0625
- lengths: int32 [1], replicated, may hold values from 1 to 4096
- stretch_owner: int32 [8], replicated, may hold values from 0 to 7, as said below
- home_replica: int32 [1], replicated, may hold values from 0 to 7, as said below
Outputs:
- mixed: bfloat16 [4096, 4096], P(('sp', 'tp'))
- cache_keys: bfloat16 [32768, 1024], P('sp', 'tp')
- home_cache_values: bfloat16 [32768, 1024], P('sp', 'tp')
Inputs may be any that keep to these rules, and one draw needn't show every extreme that they name: Stretch c of prompt p stands on replica stretch_owner[p * 8 + c]; every replica appears once. `home_replica`: the prompts' home replicas are distinct; prompt 0's home is (stretch_owner[0] + 8 / 2) modulo 8.
All inputs are finite; a program needn't handle non-finite values.
Results may differ from a plain program's by a relative error of at most 0.014.
Values may be sent and summed in bfloat16 or wider, within the bound.
A program may use at most 128 MiB of HBM per device.

v0:
```python
import functools
import math

import jax
import jax.numpy as jnp
from jax import lax
from jax.experimental import pallas as pl
from jax.experimental.pallas import tpu as pltpu
from jax.sharding import PartitionSpec as P

HEAD_DIM = 128
MAX_STRETCHES = 8
ROW_BLOCK = 512
UNROLL = 4
LOG2E = math.log2(math.e)
FAR = -1e30
MESH = pl.DeviceIdType.MESH


def find(table, value):
    index = jnp.int32(0)
    for j in range(table.shape[0]):
        index = index + jnp.where(table[j] == value, j, 0)
    return index


def attend_kernel(
    stretch, heads, owner_ref, length_ref, home_ref, q_ref, k_ref, v_ref, o_ref, kc_ref, vc_ref,
    stage, sems, top_ref, high_ref, acc_ref, vt_ref, score_ref,
):
    me = lax.axis_index("sp")
    mine = find(owner_ref, me)
    prompt = mine // MAX_STRETCHES
    own = mine % MAX_STRETCHES
    length = length_ref[prompt]
    lanes = q_ref.shape[0]
    group, block, turn = pl.program_id(0), pl.program_id(1), pl.program_id(2)
    columns = pl.ds(pl.multiple_of(group * HEAD_DIM, HEAD_DIM), HEAD_DIM)
    copies = [
        pltpu.make_async_copy(stage.at[i], out.at[:, columns], sems.at[i])
        for i, out in enumerate((kc_ref, vc_ref))
    ]

    @pl.when((block == 0) & (turn == 0))
    def _():
        homed = jnp.int32(0)
        kept = jnp.int32(0)
        for p in range(home_ref.shape[0]):
            here = home_ref[p] == me
            homed = jnp.where(here, p, homed)
            kept = jnp.where(here, length_ref[p], kept)

        def fill(j, _):
            start = pl.multiple_of(owner_ref[homed * MAX_STRETCHES + j] * stretch, stretch)
            target = pl.ds(pl.multiple_of(j * stretch, stretch), stretch)
            position = j * stretch + lax.broadcasted_iota(jnp.int32, (stretch, HEAD_DIM), 0)
            for i, source in enumerate((k_ref, v_ref)):
                block = source[pl.ds(start, stretch), :]
                stage[i, target, :] = jnp.where(position < kept, block, jnp.zeros_like(block))
            return 0

        lax.fori_loop(0, MAX_STRETCHES, fill, 0)
        for copy in copies:
            copy.start()

        def turned(j, _):
            rows = pl.ds(pl.multiple_of(j * stretch, stretch), stretch)
            vt_ref[:HEAD_DIM, rows] = v_ref[rows, :].T
            return 0

        lax.fori_loop(0, v_ref.shape[0] // stretch, turned, 0)
        vt_ref[HEAD_DIM:, :] = jnp.ones((16, v_ref.shape[0]), jnp.bfloat16)

    within = block * lanes + lax.broadcasted_iota(jnp.int32, (1, lanes), 1)
    live = own * stretch + block * lanes < length

    @pl.when(live)
    def _():
        scale = HEAD_DIM ** (-0.5) * LOG2E
        piece = stretch // 2

        def first_row(j):
            return pl.multiple_of(owner_ref[prompt * MAX_STRETCHES + j] * stretch, stretch)

        def score(j, u, c):
            rows = pl.ds(first_row(j) + c * piece, piece)
            query = q_ref[:, u * HEAD_DIM : (u + 1) * HEAD_DIM]
            scores = lax.dot_general(
                k_ref[rows, :], query, (((1,), (1,)), ((), ())), preferred_element_type=jnp.float32
            )
            score_ref[u, c * piece : (c + 1) * piece, :] = scores
            return jnp.max(scores, axis=0, keepdims=True)

        def score_all(j, u):
            highest = [score(j, u, c) for c in range(2)]
            high_ref[u] = functools.reduce(jnp.maximum, highest)

        def spread(j, u, masked, ahead):
            top = top_ref[u]
            start = first_row(j)
            if masked:
                def seen(c):
                    place_of = c * piece + lax.broadcasted_iota(jnp.int32, (piece, lanes), 0)
                    part = score_ref[u, c * piece : (c + 1) * piece, :]
                    return jnp.where(place_of <= within, part, FAR)

                high = functools.reduce(
                    jnp.maximum,
                    [jnp.max(seen(c), axis=0, keepdims=True) for c in range(2)],
                )
            else:
                def seen(c):
                    return score_ref[u, c * piece : (c + 1) * piece, :]

                high = high_ref[u]
            new_top = jnp.maximum(top, high * scale)
            rescale = jnp.exp2(top - new_top)
            highest, weights = [], []
            acc = acc_ref[u] * rescale
            for c in range(2):
                if ahead is not None:
                    highest.append(score(ahead[0], ahead[1], c))
                weights.append(jnp.exp2(seen(c) * scale - new_top).astype(jnp.bfloat16))
            acc = acc + jnp.dot(
                vt_ref[:, pl.ds(start, stretch)], jnp.concatenate(weights, axis=0),
                preferred_element_type=jnp.float32,
            )
            acc_ref[u] = acc
            top_ref[u] = new_top
            if ahead is not None:
                high_ref[ahead[1]] = functools.reduce(jnp.maximum, highest)

        top_ref[...] = jnp.full_like(top_ref, FAR)
        acc_ref[...] = jnp.zeros_like(acc_ref)
        score_all(0, 0)

        def body(j, _):
            for u in range(heads):
                spread(j, u, False, (j, u + 1) if u + 1 < heads else (j + 1, 0))
            return 0

        lax.fori_loop(0, own, body, 0)
        for u in range(heads):
            spread(own, u, True, (own, u + 1) if u + 1 < heads else None)
        alive = (own * stretch + within < length).astype(jnp.float32)
        for u in range(heads):
            out = (acc_ref[u, :HEAD_DIM] * (alive / acc_ref[u, HEAD_DIM : HEAD_DIM + 1])).T
            o_ref[:, u * HEAD_DIM : (u + 1) * HEAD_DIM] = out.astype(jnp.bfloat16)

    @pl.when(jnp.logical_not(live))
    def _():
        o_ref[...] = jnp.zeros_like(o_ref)

    @pl.when((block == pl.num_programs(1) - 1) & (turn == pl.num_programs(2) - 1))
    def _():
        for copy in copies:
            copy.wait()


def attend(stretch, tables, queries, keys, values):
    width = queries.shape[1]
    kv_width = keys.shape[1]
    local_kv = kv_width // HEAD_DIM
    group_size = width // kv_width
    heads = math.gcd(UNROLL, group_size)
    turns = group_size // heads
    lanes = math.gcd(ROW_BLOCK, stretch)
    span = MAX_STRETCHES * stretch
    cache = jax.ShapeDtypeStruct((span, kv_width), jnp.bfloat16)
    query_spec = pl.BlockSpec((lanes, heads * HEAD_DIM), lambda g, r, u, *_: (r, g * turns + u))
    kv_spec = pl.BlockSpec((keys.shape[0], HEAD_DIM), lambda g, r, u, *_: (0, g))
    return pl.pallas_call(
        functools.partial(attend_kernel, stretch, heads),
        out_shape=[jax.ShapeDtypeStruct((stretch, width), jnp.bfloat16), cache, cache],
        grid_spec=pltpu.PrefetchScalarGridSpec(
            num_scalar_prefetch=3,
            grid=(local_kv, stretch // lanes, turns),
            in_specs=[query_spec, kv_spec, kv_spec],
            out_specs=[query_spec] + [pl.BlockSpec(memory_space=pl.ANY)] * 2,
            scratch_shapes=[
                pltpu.VMEM((2, span, HEAD_DIM), jnp.bfloat16),
                pltpu.SemaphoreType.DMA((2,)),
                pltpu.VMEM((heads, 1, lanes), jnp.float32),
                pltpu.VMEM((heads, 1, lanes), jnp.float32),
                pltpu.VMEM((heads, HEAD_DIM + 16, lanes), jnp.float32),
                pltpu.VMEM((HEAD_DIM + 16, values.shape[0]), jnp.bfloat16),
                pltpu.VMEM((heads, stretch, lanes), jnp.float32),
            ],
        ),
        compiler_params=pltpu.CompilerParams(
            dimension_semantics=("arbitrary",) * 3, vmem_limit_bytes=48 * 2**20
        ),
        name="attend",
    )(*tables, queries, keys, values)


def gather_kernel(k_ref, v_ref, all_k, all_v, place_sem, send_sem, recv_sem):
    me = lax.axis_index("sp")
    rows = k_ref.shape[0]
    y, x, core = me // 4, me // 2 % 2, me % 2
    index = lambda y, x, core: y * 4 + x * 2 + core
    beside = index(y, 1 - x, core)
    above = index(1 - y, x, core)
    across = index(1 - y, 1 - x, core)
    partner = index(y, x, 1 - core)
    relay_from = core * beside + (1 - core) * above
    relay_to = core * above + (1 - core) * beside
    sources, outs = (k_ref, v_ref), (all_k, all_v)

    barrier = pltpu.get_barrier_semaphore()
    for other in (beside, above, partner):
        pl.semaphore_signal(barrier, inc=1, device_id={"sp": other}, device_id_type=MESH)
    pl.semaphore_wait(barrier, 3)

    def part(ref, owner):
        return ref.at[pl.ds(pl.multiple_of(owner * rows, rows), rows), :]

    def send(i, lane, source, owner, target):
        return pltpu.make_async_remote_copy(
            src_ref=source,
            dst_ref=part(outs[i], owner),
            send_sem=send_sem.at[lane, i],
            recv_sem=recv_sem.at[lane, i],
            device_id={"sp": target},
            device_id_type=MESH,
        )

    sent = []
    for i in range(2):
        for lane, target in ((0, beside), (1, above), (2, partner)):
            copy = send(i, lane, sources[i], me, target)
            copy.start()
            sent.append(copy)
        own = pltpu.make_async_copy(sources[i], part(outs[i], me), place_sem.at[i])
        own.start()
    relays = []
    for i in range(2):
        sent[3 * i].wait_recv()
        sent[3 * i + 1].wait_recv()
        relay = send(i, 3, part(outs[i], relay_from), relay_from, relay_to)
        relay.start()
        relays.append(relay)
        for lane, owner in ((4, beside), (5, above)):
            copy = send(i, lane, part(outs[i], owner), owner, partner)
            copy.start()
            relays.append(copy)
    last = []
    for i in range(2):
        relays[3 * i].wait_recv()
        copy = send(i, 6, part(outs[i], across), across, partner)
        copy.start()
        last.append(copy)
    for i in range(2):
        sent[3 * i + 2].wait_recv()
        relays[3 * i + 1].wait_recv()
        relays[3 * i + 2].wait_recv()
        last[i].wait_recv()
        pltpu.make_async_copy(sources[i], part(outs[i], me), place_sem.at[i]).wait()
    for copy in sent + relays + last:
        copy.wait_send()


def gather(keys, values):
    replicas = lax.axis_size("sp")
    if replicas != 8:
        return (
            lax.all_gather(keys, "sp", axis=0, tiled=True),
            lax.all_gather(values, "sp", axis=0, tiled=True),
        )
    shape = jax.ShapeDtypeStruct((replicas * keys.shape[0], keys.shape[1]), keys.dtype)
    return pl.pallas_call(
        gather_kernel,
        out_shape=[shape] * 2,
        in_specs=[pl.BlockSpec(memory_space=pltpu.VMEM)] * 2,
        out_specs=[pl.BlockSpec(memory_space=pl.ANY)] * 2,
        scratch_shapes=[
            pltpu.SemaphoreType.DMA((2,)),
            pltpu.SemaphoreType.DMA((7, 2)),
            pltpu.SemaphoreType.DMA((7, 2)),
        ],
        compiler_params=pltpu.CompilerParams(collective_id=0, has_side_effects=True),
        name="gather",
    )(keys, values)


def project_kernel(
    steps, a_ref, w_ref, o_ref, work, own, out_far, out_near, out_sum,
    in_far, in_near, in_sum, send_sem, recv_sem,
):
    me = lax.axis_index("tp")
    n = 4
    rows = a_ref.shape[0] // n
    step = pl.program_id(0)

    def hops(j):
        turn = 1 - 2 * (j % 2)
        return (me + turn + n) % n, (me - turn + n) % n

    def send(kind, j, target):
        source, dest = ((out_far, in_far), (out_near, in_near), (out_sum, in_sum))[kind]
        return pltpu.make_async_remote_copy(
            src_ref=source.at[j],
            dst_ref=dest.at[j],
            send_sem=send_sem.at[kind, j],
            recv_sem=recv_sem.at[kind, j],
            device_id={"tp": target},
            device_id_type=MESH,
        )

    @pl.when(step == 0)
    def _():
        barrier = pltpu.get_barrier_semaphore()
        for other in ((me + 1) % n, (me + n - 1) % n):
            pl.semaphore_signal(barrier, inc=1, device_id={"tp": other}, device_id_type=MESH)
        pl.semaphore_wait(barrier, 2)

    def rows_of(device):
        return pl.ds(pl.multiple_of(device * rows, rows), rows)

    def relay(j):
        toward, away = hops(j)
        send(0, j, toward).wait_recv()
        total = work[j % 2, rows_of(toward), :] + in_far[j].astype(jnp.float32)
        out_sum[j] = total.astype(jnp.bfloat16)
        send(2, j, toward).start()

    toward, away = hops(step)
    work[step % 2] = jnp.dot(a_ref[...], w_ref[...], preferred_element_type=jnp.float32)
    out_far[step] = work[step % 2, rows_of((me + 2) % n), :].astype(jnp.bfloat16)
    send(0, step, toward).start()
    out_near[step] = work[step % 2, rows_of(away), :].astype(jnp.bfloat16)
    send(1, step, away).start()
    own[step] = work[step % 2, rows_of(me), :]

    @pl.when(step > 0)
    def _():
        relay(step - 1)

    @pl.when(step == steps - 1)
    def _():
        relay(step)
        width = o_ref.shape[1] // steps
        for j in range(steps):
            toward, away = hops(j)
            send(1, j, away).wait_recv()
            send(2, j, toward).wait_recv()
            total = own[j] + in_near[j].astype(jnp.float32) + in_sum[j].astype(jnp.float32)
            o_ref[:, j * width : (j + 1) * width] = total.astype(jnp.bfloat16)
        for j in range(steps):
            toward, away = hops(j)
            send(0, j, toward).wait_send()
            send(1, j, away).wait_send()
            send(2, j, toward).wait_send()


def project(attended, w_out):
    if lax.axis_size("tp") != 4:
        partial = jnp.dot(attended, w_out, preferred_element_type=jnp.float32)
        return lax.psum_scatter(
            partial.astype(jnp.bfloat16), "tp", scatter_dimension=0, tiled=True
        )
    tokens, depth = attended.shape
    features = w_out.shape[1]
    rows = tokens // 4
    steps = 8
    width = features // steps
    buffer = pltpu.VMEM((steps, rows, width), jnp.bfloat16)
    return pl.pallas_call(
        functools.partial(project_kernel, steps),
        out_shape=jax.ShapeDtypeStruct((rows, features), jnp.bfloat16),
        grid=(steps,),
        in_specs=[
            pl.BlockSpec((tokens, depth), lambda j: (0, 0)),
            pl.BlockSpec((depth, width), lambda j: (0, j)),
        ],
        out_specs=pl.BlockSpec((rows, features), lambda j: (0, 0)),
        scratch_shapes=[
            pltpu.VMEM((2, tokens, width), jnp.float32),
            pltpu.VMEM((steps, rows, width), jnp.float32),
            buffer, buffer, buffer, buffer, buffer, buffer,
            pltpu.SemaphoreType.DMA((3, steps)),
            pltpu.SemaphoreType.DMA((3, steps)),
        ],
        compiler_params=pltpu.CompilerParams(
            collective_id=1,
            has_side_effects=True,
            dimension_semantics=("arbitrary",),
            vmem_limit_bytes=48 * 2**20,
        ),
        name="project",
    )(attended, w_out)


def shards(queries, keys, values, w_out, lengths, stretch_owner, home_replica):
    stretch = queries.shape[0]
    tables = (stretch_owner, lengths, home_replica)
    all_keys, all_values = gather(keys, values)
    attended, kept_keys, kept_values = attend(stretch, tables, queries, all_keys, all_values)
    return (project(attended, w_out), kept_keys, kept_values)


def solution(mesh):
    placed = (P("sp", "tp"), P("sp", "tp"), P("sp", "tp"), P("tp", None), P(), P(), P())
    return jax.shard_map(
        shards,
        mesh=mesh,
        in_specs=placed,
        out_specs=(P(("sp", "tp"), None), P("sp", "tp"), P("sp", "tp")),
        check_vma=False,
    )
```

profile of v0, /device:TPU:0, one launch (start us, length us, event | category | flops | bytes accessed | tf_op | source)
XLA Modules:
  0.0 113.9 jit_solution(2032984611907614605)
XLA Ops:
  1.9 25.4 %gather.1 = (bf16[4096,256]{1,0:T(8,128)(2,1)}, bf16[4096,256]{1,0:T(8,128)(2,1)}) custom-call(bf16[512,256]{1,0:T(8,128)(2,1)} %k_ref.1, bf16[512,256]{1,0:T(8,128)(2,1)} %v_ref.1), custom_call_target="tpu_custom_call" | custom-call | tf_op jit(solution)/shard_map/gather/pallas_call | solution.py:271
  27.3 0.0 copy-start
  27.3 1.6 %copy-done = bf16[512,2048]{1,0:T(8,128)(2,1)S(1)} copy-done((bf16[512,2048]{1,0:T(8,128)(2,1)S(1)}, bf16[512,2048]{1,0:T(8,128)(2,1)}, u32[]{:S(2)}) %copy-start) | copy-done | bytes 2097176
  28.9 0.0 copy-start.1
  28.9 0.7 copy-done.1
  29.6 7.3 %attend.1 = (bf16[512,2048]{1,0:T(8,128)(2,1)S(1)}, bf16[4096,256]{1,0:T(8,128)(2,1)}, bf16[4096,256]{1,0:T(8,128)(2,1)}) custom-call(s32[8]{0:T(128)S(1)} %copy-done.1, s32[1]{0:T(128)S(6)} %copy.11.length_ref, s32[1]{0:T(128)S(6)} %copy.12.home_ref, bf16[512,2048]{1,0:T(8,128)(2,1)S(1)} %copy-done, bf16[4096,256]{1,0:T(8,128)(2,1)} %get-tuple-element.8.k_ref, ...), custom_call_target="tpu_custom_call" | custom-call | tf_op jit(solution)/shard_map/attend/pallas_call | solution.py:172
  36.8 76.1 %project.1 = bf16[128,4096]{1,0:T(8,128)(2,1)S(1)} custom-call(bf16[512,2048]{1,0:T(8,128)(2,1)S(1)} %get-tuple-element.10.a_ref, bf16[2048,4096]{1,0:T(8,128)(2,1)} %w_ref.1), custom_call_target="tpu_custom_call" | custom-call | tf_op jit(solution)/shard_map/project/pallas_call | solution.py:368
  112.9 1.0 copy.13
Async XLA Ops:
  27.3 1.6 %copy-start = (bf16[512,2048]{1,0:T(8,128)(2,1)S(1)}, bf16[512,2048]{1,0:T(8,128)(2,1)}, u32[]{:S(2)}) copy-start(bf16[512,2048]{1,0:T(8,128)(2,1)} %q_ref.1) | copy-start | bytes 6291460
  28.9 0.7 copy-start.1
where the time goes:
time: 114 us
  Pallas kernels  109 us (96%)
  local copies, waits for them, and re-layouts  3.21 us (3%)
  between operations  1.96 us (2%)
    pallas_call x1, Pallas kernels, project(): pl.pallas_call(functools.partial(project_kernel, steps), out_shape=jax.Sh...  76.1 us
    pallas_call x1, Pallas kernels, gather(): pl.pallas_call(gather_kernel, out_shape=[shape] * 2, in_specs=[pl.BlockSp...  25.4 us
    pallas_call x1, Pallas kernels, attend(): pl.pallas_call(functools.partial(attend_kernel, stretch, heads), out_shap...  7.26 us
    unnamed x5, local copies, waits for them, and re-layouts  3.21 us

commit v1 on v0

--- a/solution.py
+++ b/solution.py
@@ -284,26 +284,20 @@
 
 
 def project_kernel(
-    steps, a_ref, w_ref, o_ref, work, own, out_far, out_near, out_sum,
-    in_far, in_near, in_sum, send_sem, recv_sem,
+    steps, a_ref, w_ref, o_ref, work, own, out, from_left, from_right, send_sem, left_sem, right_sem
 ):
     me = lax.axis_index("tp")
     n = 4
     rows = a_ref.shape[0] // n
     step = pl.program_id(0)
 
-    def hops(j):
-        turn = 1 - 2 * (j % 2)
-        return (me + turn + n) % n, (me - turn + n) % n
-
-    def send(kind, j, target):
-        source, dest = ((out_far, in_far), (out_near, in_near), (out_sum, in_sum))[kind]
+    def push(j, part, up):
         return pltpu.make_async_remote_copy(
-            src_ref=source.at[j],
-            dst_ref=dest.at[j],
-            send_sem=send_sem.at[kind, j],
-            recv_sem=recv_sem.at[kind, j],
-            device_id={"tp": target},
+            src_ref=out.at[j, part],
+            dst_ref=(from_left if up else from_right).at[j, part],
+            send_sem=send_sem.at[j, part],
+            recv_sem=(left_sem if up else right_sem).at[j, part],
+            device_id={"tp": (me + 1) % n if up else (me + n - 1) % n},
             device_id_type=MESH,
         )
 
@@ -314,43 +308,79 @@
             pl.semaphore_signal(barrier, inc=1, device_id={"tp": other}, device_id_type=MESH)
         pl.semaphore_wait(barrier, 2)
 
-    def rows_of(device):
-        return pl.ds(pl.multiple_of(device * rows, rows), rows)
-
-    def relay(j):
-        toward, away = hops(j)
-        send(0, j, toward).wait_recv()
-        total = work[j % 2, rows_of(toward), :] + in_far[j].astype(jnp.float32)
-        out_sum[j] = total.astype(jnp.bfloat16)
-        send(2, j, toward).start()
-
-    toward, away = hops(step)
+    def piece(j, part):
+        return work[j % 2, part * rows : (part + 1) * rows, :]
+
+    def relay(j, up):
+        for part in range(n - 1, 1, -1) if up else range(n - 2):
+
+            @pl.when((me < part) if up else (me > part))
+            def _():
+                push(j, part, up).wait_recv()
+                before = (from_left if up else from_right)[j, part]
+                out[j, part] = (piece(j, part) + before.astype(jnp.float32)).astype(jnp.bfloat16)
+                push(j, part, up).start()
+
+    def relays(j):
+        @pl.when((me > 0) & (2 * me < n))
+        def _():
+            relay(j, True)
+            relay(j, False)
+
+        @pl.when((me < n - 1) & (2 * me >= n))
+        def _():
+            relay(j, False)
+            relay(j, True)
+
     work[step % 2] = jnp.dot(a_ref[...], w_ref[...], preferred_element_type=jnp.float32)
-    out_far[step] = work[step % 2, rows_of((me + 2) % n), :].astype(jnp.bfloat16)
-    send(0, step, toward).start()
-    out_near[step] = work[step % 2, rows_of(away), :].astype(jnp.bfloat16)
-    send(1, step, away).start()
-    own[step] = work[step % 2, rows_of(me), :]
+    own[step] = work[step % 2, pl.ds(pl.multiple_of(me * rows, rows), rows), :]
+
+    @pl.when(me == 0)
+    def _():
+        for part in range(n - 1, 0, -1):
+            out[step, part] = piece(step, part).astype(jnp.bfloat16)
+            push(step, part, True).start()
+
+    @pl.when(me == n - 1)
+    def _():
+        for part in range(n - 1):
+            out[step, part] = piece(step, part).astype(jnp.bfloat16)
+            push(step, part, False).start()
 
     @pl.when(step > 0)
     def _():
-        relay(step - 1)
+        relays(step - 1)
 
     @pl.when(step == steps - 1)
     def _():
-        relay(step)
+        relays(step)
+
+        @pl.when(me > 0)
+        def _():
+            for j in range(steps):
+                push(j, me, True).wait_recv()
+                own[j] = own[j] + from_left[j, me].astype(jnp.float32)
+
+        @pl.when(me < n - 1)
+        def _():
+            for j in range(steps):
+                push(j, me, False).wait_recv()
+                own[j] = own[j] + from_right[j, me].astype(jnp.float32)
+
         width = o_ref.shape[1] // steps
         for j in range(steps):
-            toward, away = hops(j)
-            send(1, j, away).wait_recv()
-            send(2, j, toward).wait_recv()
-            total = own[j] + in_near[j].astype(jnp.float32) + in_sum[j].astype(jnp.float32)
-            o_ref[:, j * width : (j + 1) * width] = total.astype(jnp.bfloat16)
-        for j in range(steps):
-            toward, away = hops(j)
-            send(0, j, toward).wait_send()
-            send(1, j, away).wait_send()
-            send(2, j, toward).wait_send()
+            o_ref[:, j * width : (j + 1) * width] = own[j].astype(jnp.bfloat16)
+        for part in range(n):
+
+            @pl.when(me < part)
+            def _():
+                for j in range(steps):
+                    push(j, part, True).wait_send()
+
+            @pl.when(me > part)
+            def _():
+                for j in range(steps):
+                    push(j, part, False).wait_send()
 
 
 def project(attended, w_out):
@@ -364,7 +394,7 @@
     rows = tokens // 4
     steps = 8
     width = features // steps
-    buffer = pltpu.VMEM((steps, rows, width), jnp.bfloat16)
+    buffer = pltpu.VMEM((steps, 4, rows, width), jnp.bfloat16)
     return pl.pallas_call(
         functools.partial(project_kernel, steps),
         out_shape=jax.ShapeDtypeStruct((rows, features), jnp.bfloat16),
@@ -377,9 +407,10 @@
         scratch_shapes=[
             pltpu.VMEM((2, tokens, width), jnp.float32),
             pltpu.VMEM((steps, rows, width), jnp.float32),
-            buffer, buffer, buffer, buffer, buffer, buffer,
-            pltpu.SemaphoreType.DMA((3, steps)),
-            pltpu.SemaphoreType.DMA((3, steps)),
+            buffer, buffer, buffer,
+            pltpu.SemaphoreType.DMA((steps, 4)),
+            pltpu.SemaphoreType.DMA((steps, 4)),
+            pltpu.SemaphoreType.DMA((steps, 4)),
         ],
         compiler_params=pltpu.CompilerParams(
             collective_id=1,

time: 114 us -> 123 us (1.079)
  the two profiles are of different devices: /device:TPU:0 before, /device:TPU:4 now
where the time goes in v1:
time: 123 us
  Pallas kernels  118 us (96%)
  local copies, waits for them, and re-layouts  3.21 us (3%)
  between operations  1.96 us (2%)
    pallas_call x1, Pallas kernels, project(): pl.pallas_call(functools.partial(project_kernel, steps), out_shape=jax.Sh...  71.8 us
    pallas_call x1, Pallas kernels, gather(): pl.pallas_call(gather_kernel, out_shape=[shape] * 2, in_specs=[pl.BlockSp...  23.9 us
    pallas_call x1, Pallas kernels, attend(): pl.pallas_call(functools.partial(attend_kernel, stretch, heads), out_shap...  22.1 us
    unnamed x5, local copies, waits for them, and re-layouts  3.21 us

profile of v1, /device:TPU:4, one launch (start us, length us, event | category | flops | bytes accessed | tf_op | source)
XLA Modules:
  0.0 123.0 jit_solution(14612326611975391032)
XLA Ops:
  1.9 23.9 %gather.1 = (bf16[4096,256]{1,0:T(8,128)(2,1)}, bf16[4096,256]{1,0:T(8,128)(2,1)}) custom-call(bf16[512,256]{1,0:T(8,128)(2,1)} %k_ref.1, bf16[512,256]{1,0:T(8,128)(2,1)} %v_ref.1), custom_call_target="tpu_custom_call" | custom-call | tf_op jit(solution)/shard_map/gather/pallas_call | solution.py:271
  25.8 0.0 copy-start
  25.8 1.6 %copy-done = bf16[512,2048]{1,0:T(8,128)(2,1)S(1)} copy-done((bf16[512,2048]{1,0:T(8,128)(2,1)S(1)}, bf16[512,2048]{1,0:T(8,128)(2,1)}, u32[]{:S(2)}) %copy-start) | copy-done | bytes 2097176
  27.4 0.0 copy-start.1
  27.4 0.7 copy-done.1
  28.1 22.1 %attend.1 = (bf16[512,2048]{1,0:T(8,128)(2,1)S(1)}, bf16[4096,256]{1,0:T(8,128)(2,1)}, bf16[4096,256]{1,0:T(8,128)(2,1)}) custom-call(s32[8]{0:T(128)S(1)} %copy-done.1, s32[1]{0:T(128)S(6)} %copy.11.length_ref, s32[1]{0:T(128)S(6)} %copy.12.home_ref, bf16[512,2048]{1,0:T(8,128)(2,1)S(1)} %copy-done, bf16[4096,256]{1,0:T(8,128)(2,1)} %get-tuple-element.8.k_ref, ...), custom_call_target="tpu_custom_call" | custom-call | tf_op jit(solution)/shard_map/attend/pallas_call | solution.py:172
  50.2 71.8 %project.1 = bf16[128,4096]{1,0:T(8,128)(2,1)S(1)} custom-call(bf16[512,2048]{1,0:T(8,128)(2,1)S(1)} %get-tuple-element.10.a_ref, bf16[2048,4096]{1,0:T(8,128)(2,1)} %w_ref.1), custom_call_target="tpu_custom_call" | custom-call | tf_op jit(solution)/shard_map/project/pallas_call | solution.py:398
  122.0 1.0 copy.13
Async XLA Ops:
  25.8 1.6 %copy-start = (bf16[512,2048]{1,0:T(8,128)(2,1)S(1)}, bf16[512,2048]{1,0:T(8,128)(2,1)}, u32[]{:S(2)}) copy-start(bf16[512,2048]{1,0:T(8,128)(2,1)} %q_ref.1) | copy-start | bytes 6291460
  27.4 0.7 copy-start.1
